TPU v7x, 32 devices: a whole 2x2x4 slice. The times are simulated.
32 devices in a mesh: grp: 8 (over z, core), rep: 4 (over y, x).
Axes of the slice: x: 2, y: 2, z: 4, core: 2. Of those that a mesh axis runs over, the one named last changes fastest.
Arguments:
- queries: bfloat16 [12288, 2560], P(('grp', 'rep')), may hold values from -60 to 60
- passages: bfloat16 [65536, 2560], P(('grp', 'rep')), may hold values from -60 to 60
- block_valid_counts: int32 [512], P(('grp', 'rep')), may hold values from 16 to 128
- positive_index: int32 [12288], P(('grp', 'rep')), may hold values from 0 to 2047, as said below
- neg_blocks: int32 [32, 12], P(('grp', 'rep')), may hold values from 0 to 511, as said below
- query_weights: float32 [12288], P(('grp', 'rep')), may hold values from 0.3 to 10
Outputs:
- query_loss: float32 [12288], P(('grp', 'rep'))
- mean_loss: float32 [], replicated
Inputs may be any that keep to these rules, and one draw needn't show every extreme that they name: `neg_blocks`: row g lists 12 distinct blocks, all owned by query groups with the same rep index as group g and another grp index; at most 2 of them belong to one group, and some group gives exactly 2 in every row. `positive_index`: always a valid row of one of the query's own group's blocks.
All inputs are finite; a program needn't handle non-finite values.
Results may differ from a plain program's by a relative error of at most 0.0003.
Values may be sent and summed in bfloat16 or wider, within the bound.
A program may use at most 256 MiB of HBM per device.

v0:
```python
import jax
import jax.numpy as jnp
from jax import lax
from jax.sharding import PartitionSpec as P

CAP = 2
inverse_softmax_sharpness = 20.0
norm_epsilon = 1e-06


def normalize(rows):
    values = rows.astype(jnp.float32)
    scale = lax.rsqrt(jnp.sum(values * values, axis=-1, keepdims=True) + norm_epsilon)
    return (values * scale).astype(jnp.bfloat16)


def local(queries, passages, block_valid_counts, positive_index, neg_blocks, query_weights):
    group_count = lax.axis_size("grp")
    replica_count = lax.axis_size("rep")
    local_rows = passages.shape[0]
    blocks_here = block_valid_counts.shape[0]
    block_rows = local_rows // blocks_here
    feature_width = passages.shape[1]
    question_unit_vectors = normalize(queries)
    document_unit_vectors = normalize(passages)
    row_valid = jnp.arange(local_rows, dtype=jnp.int32) % block_rows < jnp.repeat(
        block_valid_counts, block_rows
    )
    shared_pool_similarity = (
        lax.dot_general(
            question_unit_vectors,
            document_unit_vectors,
            (((1,), (1,)), ((), ())),
            preferred_element_type=jnp.float32,
        )
        * inverse_softmax_sharpness
    )
    local_total = jnp.sum(
        jnp.where(row_valid[None, :], jnp.exp(shared_pool_similarity), 0.0), axis=1
    )
    positive_score = jnp.take_along_axis(shared_pool_similarity, positive_index[:, None], axis=1)[
        :, 0
    ]
    wanted = neg_blocks[0]
    owner_device = wanted // blocks_here
    owner_group = owner_device // replica_count
    local_block = wanted % blocks_here
    listed = wanted.shape[0]
    same_owner = owner_group[:, None] == owner_group[None, :]
    earlier_slot = jnp.arange(listed)[:, None] > jnp.arange(listed)[None, :]
    slot_rank = jnp.sum(jnp.logical_and(same_owner, earlier_slot), axis=1)
    requests = (
        jnp.full((group_count, CAP), -1, jnp.int32).at[owner_group, slot_rank].set(local_block)
    )
    incoming = lax.all_to_all(requests, "grp", split_axis=0, concat_axis=0, tiled=True)
    requested = incoming >= 0
    safe_block = jnp.maximum(incoming, 0)
    matches = safe_block[:, :, None] == jnp.arange(blocks_here, dtype=jnp.int32)[None, None, :]
    slot_counts = jnp.where(
        requested, jnp.sum(jnp.where(matches, block_valid_counts[None, None, :], 0), axis=2), 0
    )
    unit_blocks = document_unit_vectors.reshape(blocks_here, block_rows, feature_width)
    picked = unit_blocks[safe_block]
    arrived = lax.all_to_all(picked, "grp", split_axis=0, concat_axis=0, tiled=True)
    kept_counts = lax.all_to_all(slot_counts, "grp", split_axis=0, concat_axis=0, tiled=True)
    similarity = (
        jnp.einsum(
            "qd,skrd->kqsr", question_unit_vectors, arrived, preferred_element_type=jnp.float32
        )
        * inverse_softmax_sharpness
    )
    live_rows = jnp.arange(block_rows, dtype=jnp.int32)[None, None, :] < kept_counts[:, :, None]
    live_rows = jnp.transpose(live_rows, (1, 0, 2))[:, None]
    slot_totals = jnp.sum(jnp.where(live_rows, jnp.exp(similarity), 0.0), axis=(2, 3))
    hard_total = jnp.sum(slot_totals, axis=0)
    query_loss = jnp.log(local_total + hard_total) - positive_score
    weighted_sum, weight_sum = lax.psum(
        (jnp.sum(query_weights * query_loss), jnp.sum(query_weights)), ("grp", "rep")
    )
    return (query_loss, weighted_sum / weight_sum)


def solution(mesh):
    in_specs = (
        P(("grp", "rep"), None),
        P(("grp", "rep"), None),
        P(("grp", "rep")),
        P(("grp", "rep")),
        P(("grp", "rep"), None),
        P(("grp", "rep")),
    )
    out_specs = (P(("grp", "rep")), P())
    return jax.shard_map(local, mesh=mesh, in_specs=in_specs, out_specs=out_specs, check_vma=False)
```

profile of v0, /device:TPU:12, one launch (start us, length us, event | category | flops | bytes accessed | tf_op | source)
XLA Modules:
  0.0 324.3 jit_solution(4056627843211229691)
XLA Ops:
  0.6 0.7 fusion.21
  1.3 0.7 and_select_fusion
  2.0 0.2 convert_reduce_fusion
  2.2 0.7 fusion.22
  2.8 1.1 scatter_fusion
  4.0 0.7 copy.22
  4.6 5.3 %all-to-all-start = ((s32[8,1,2]{2,1,0:T(1,128)}), s32[8,1,2]{2,1,0:T(1,128)S(1)}, u32[]{:S(2)}, u32[]{:S(2)}) async-start(s32[8,1,2]{2,1,0:T(1,128)} %copy.22), calls=%async_computation | async-start | bytes 8192 | tf_op jit(solution)/shard_map/all_to_all | solution.py:55
  10.0 6.2 %fusion = f32[2048]{0:T(1024)S(1)} fusion(bf16[2048,2560]{1,0:T(8,128)(2,1)} %param.7), kind=kLoop, calls=%fused_computation.5 | loop fusion | flops 15726592 | bytes 10493952 | tf_op jit(solution)/shard_map/reduce_sum | solution.py:13
  16.2 0.7 copy-done
  16.9 5.5 %fusion.1 = bf16[2048,2560]{1,0:T(8,128)(2,1)} fusion(bf16[2048,2560]{1,0:T(8,128)(2,1)S(1)} %copy-done, f32[2048]{0:T(1024)S(1)} %add_rsqrt_fusion), kind=kLoop, calls=%fused_computation.6 | loop fusion | flops 15728640 | bytes 20979712 | tf_op jit(solution)/shard_map/convert_element_type | solution.py:14
  22.5 0.2 select_reduce_fusion.1
  22.7 0.7 copy.25
  23.5 0.1 reshape.238
  23.6 5.1 %all-to-all-start.1 = ((s32[8,1,2]{2,1,0:T(1,128)}), s32[8,1,2]{2,1,0:T(1,128)S(1)}, u32[]{:S(2)}, u32[]{:S(2)}) async-start(s32[8,1,2]{2,1,0:T(1,128)} %copy.25), calls=%async_computation.1 | async-start | bytes 8192 | tf_op jit(solution)/shard_map/all_to_all | solution.py:65
  28.7 9.6 %gather_fusion = bf16[16,128,2560]{2,1,0:T(8,128)(2,1)} fusion(bf16[16,128,2560]{2,1,0:T(8,128)(2,1)} %bitcast.68, s32[1024]{0:T(1024)S(1)} %pad_clamp_fusion), kind=kCustom, calls=%fused_computation | custom fusion | bytes 20971584 | tf_op jit(solution)/shard_map/gather | solution.py:63
  38.3 5.2 %all-to-all-start.2 = ((bf16[8,2,128,2560]{3,2,1,0:T(8,128)(2,1)}), bf16[8,2,128,2560]{3,2,1,0:T(8,128)(2,1)}, u32[]{:S(2)}, u32[]{:S(2)}) async-start(bf16[8,2,128,2560]{3,2,1,0:T(8,128)(2,1)} %bitcast.69), calls=%async_computation.2 | async-start | bytes 20971520 | tf_op jit(solution)/shard_map/all_to_all | solution.py:64
  43.7 0.5 fusion.2
  44.1 9.9 %select_reduce_fusion = (f32[384]{0:T(512)S(1)}, f32[384,2048]{1,0:T(8,128)}) fusion(pred[2048]{0:T(1024)(128)(4,1)S(1)} %fusion.11, bf16[2048,2560]{1,0:T(8,128)(2,1)} %fusion.1, bf16[384,2560]{1,0:T(8,128)(2,1)S(1)} %copy-done.1, f32[384]{0:T(512)S(1)} %add_rsqrt_fusion.1), kind=kOutput, calls=%fused_computation.13 | convolution fusion | flops 4031839744 | bytes 15602688 | tf_op jit(solution)/shard_map/dot_general | solution.py:30
  54.0 5.2 %gather_fusion.1 = f32[384]{0:T(512)S(1)} fusion(f32[384,2048]{1,0:T(8,128)} %get-tuple-element.12, s32[384]{0:T(512)S(1)} %fusion.19), kind=kCustom, calls=%fused_computation.1 | custom fusion | bytes 6144 | tf_op jit(solution)/shard_map/jit(take_along_axis)/gather | solution.py:41
  59.3 0.1 copy.27
  59.5 209.4 %all-to-all-done.2 = bf16[8,2,128,2560]{3,2,1,0:T(8,128)(2,1)} async-done(((bf16[8,2,128,2560]{3,2,1,0:T(8,128)(2,1)}), bf16[8,2,128,2560]{3,2,1,0:T(8,128)(2,1)}, u32[]{:S(2)}, u32[]{:S(2)}) %all-to-all-start.2) | async-done | bytes 10485792 | tf_op jit(solution)/shard_map/all_to_all | solution.py:64
  268.8 8.5 %fusion.4 = f32[384]{0:T(512)S(1)} fusion(pred[2,8,128]{2,0,1:T(4,128)(4,1)S(1)} %iota_compare_fusion.2, bf16[8,2,128,2560]{3,2,1,0:T(8,128)(2,1)} %all-to-all-done.2, bf16[384,2560]{1,0:T(8,128)(2,1)S(1)} %copy-done.1, f32[384]{0:T(512)S(1)} %add_rsqrt_fusion.1), kind=kOutput, calls=%fused_computation.12 | convolution fusion | flops 4031839744 | bytes 12456960 | tf_op jit(solution)/shard_map/qd,skrd->kqsr/dot_general | solution.py:67
  277.3 1.3 fusion.24
  278.6 43.4 %all-reduce = (f32[]{:T(128)}, f32[]{:T(128)}) all-reduce(f32[]{:T(128)} %get-tuple-element.3, f32[]{:T(128)} %get-tuple-element.2), channel_id=1, replica_groups=mesh['grp'=8,'rep'=4] {'grp','rep'}, use_global_device_ids=true, to_apply=%region_8.9 | all-reduce | flops 2 | bytes 16 | tf_op jit(solution)/shard_map/psum | solution.py:77
  (27 shorter events, 0.5 us)
Async XLA Ops:
  4.6 17.8 %all-to-all-start = ((s32[8,1,2]{2,1,0:T(1,128)}), s32[8,1,2]{2,1,0:T(1,128)S(1)}, u32[]{:S(2)}, u32[]{:S(2)}) async-start(s32[8,1,2]{2,1,0:T(1,128)} %copy.22), calls=%async_computation | async-start | bytes 8192 | tf_op jit(solution)/shard_map/all_to_all | solution.py:55
  10.0 7.0 %copy-start = (bf16[2048,2560]{1,0:T(8,128)(2,1)S(1)}, bf16[2048,2560]{1,0:T(8,128)(2,1)}, u32[]{:S(2)}) copy-start(bf16[2048,2560]{1,0:T(8,128)(2,1)} %param.7) | copy-start | bytes 31457284
  16.9 5.6 %copy-start.3 = (s32[16]{0:T(128)S(1)}, s32[16]{0:T(128)}, u32[]{:S(2)}) copy-start(s32[16]{0:T(128)} %param.8) | copy-start | bytes 196
  23.6 14.7 %all-to-all-start.1 = ((s32[8,1,2]{2,1,0:T(1,128)}), s32[8,1,2]{2,1,0:T(1,128)S(1)}, u32[]{:S(2)}, u32[]{:S(2)}) async-start(s32[8,1,2]{2,1,0:T(1,128)} %copy.25), calls=%async_computation.1 | async-start | bytes 8192 | tf_op jit(solution)/shard_map/all_to_all | solution.py:65
  38.2 5.2 %copy-start.2 = (s32[384]{0:T(512)S(1)}, s32[384]{0:T(512)}, u32[]{:S(2)}) copy-start(s32[384]{0:T(512)} %param.9) | copy-start | bytes 4612
  38.3 5.4 %copy-start.1 = (bf16[384,2560]{1,0:T(8,128)(2,1)S(1)}, bf16[384,2560]{1,0:T(8,128)(2,1)}, u32[]{:S(2)}) copy-start(bf16[384,2560]{1,0:T(8,128)(2,1)} %param.6) | copy-start | bytes 5898244
  38.3 230.6 %all-to-all-start.2 = ((bf16[8,2,128,2560]{3,2,1,0:T(8,128)(2,1)}), bf16[8,2,128,2560]{3,2,1,0:T(8,128)(2,1)}, u32[]{:S(2)}, u32[]{:S(2)}) async-start(bf16[8,2,128,2560]{3,2,1,0:T(8,128)(2,1)} %bitcast.69), calls=%async_computation.2 | async-start | bytes 20971520 | tf_op jit(solution)/shard_map/all_to_all | solution.py:64
  59.4 217.9 %copy-start.4 = (f32[384]{0:T(512)S(1)}, f32[384]{0:T(512)}, u32[]{:S(2)}) copy-start(f32[384]{0:T(512)} %param.11) | copy-start | bytes 4612
where the time goes:
time: 325 us; the launch traced here: 324 us
  waiting for transfers between devices  209 us (64%)
  blocking collectives  43.4 us (13%)
  matrix products  18.4 us (6%)
  local copies, waits for them, and re-layouts  18.3 us (6%)
  other arithmetic  16.1 us (5%)
  starting transfers between devices  15.7 us (5%)
    all_to_all x1, waiting for transfers between devices, local(): lax.all_to_all(picked, 'grp', split_axis=0, concat_axis=0, tiled=True)  209 us
    psum x1, blocking collectives, local(): lax.psum((jnp.sum(query_weights * query_loss), jnp.sum(query_weights)), (...  43.4 us
    dot_general x1, matrix products, local(): lax.dot_general(question_unit_vectors, document_unit_vectors, (((1,), (1,...  9.91 us
    gather x1, local copies, waits for them, and re-layouts, local(): picked = unit_blocks[safe_block]  9.57 us
    dot_general x1, matrix products, local(): jnp.einsum('qd,skrd->kqsr', question_unit_vectors, arrived, preferred_ele...  8.48 us
    reduce_sum x2, other arithmetic, normalize(): jnp.sum(values * values, axis=-1, keepdims=True) + norm_epsilon  6.69 us
  transfers between devices with their start and end apart: 3, of which 1 were waited for; matrix products, arithmetic and copies ran while one was open for 11% of the time, Pallas kernels for 0%

commit v1 on v0

--- a/solution.py
+++ b/solution.py
@@ -2,6 +2,7 @@
 import jax.numpy as jnp
 from jax import lax
 from jax.sharding import PartitionSpec as P
+from jax.lax import psum
 
 CAP = 2
 inverse_softmax_sharpness = 20.0
@@ -74,8 +75,8 @@
     slot_totals = jnp.sum(jnp.where(live_rows, jnp.exp(similarity), 0.0), axis=(2, 3))
     hard_total = jnp.sum(slot_totals, axis=0)
     query_loss = jnp.log(local_total + hard_total) - positive_score
-    weighted_sum, weight_sum = lax.psum(
-        (jnp.sum(query_weights * query_loss), jnp.sum(query_weights)), ("grp", "rep")
+    weighted_sum, weight_sum = psum(
+        psum((jnp.sum(query_weights * query_loss), jnp.sum(query_weights)), "rep"), axis_name="grp"
     )
     return (query_loss, weighted_sum / weight_sum)
 

time: 325 us -> 311 us (0.957)
  the two profiles are of different devices: /device:TPU:12 before, /device:TPU:0 now
where the time goes in v1:
time: 311 us; the launch traced here: 310 us
  waiting for transfers between devices  213 us (68%)
  blocking collectives  24.8 us (8%)
  local copies, waits for them, and re-layouts  18.4 us (6%)
  matrix products  18.4 us (6%)
  starting transfers between devices  16.7 us (5%)
  other arithmetic  16 us (5%)
  between operations  3.13 us (1%)
    all_to_all x1, waiting for transfers between devices, local(): lax.all_to_all(picked, 'grp', split_axis=0, concat_axis=0, tiled=True)  213 us
    psum x1, blocking collectives, local(): psum(psum((jnp.sum(query_weights * query_loss), jnp.sum(query_weights)),...  14.2 us
    psum x1, blocking collectives, local(): psum((jnp.sum(query_weights * query_loss), jnp.sum(query_weights)), 'rep')  10.6 us
    dot_general x1, matrix products, local(): lax.dot_general(question_unit_vectors, document_unit_vectors, (((1,), (1,...  9.91 us
    gather x1, local copies, waits for them, and re-layouts, local(): picked = unit_blocks[safe_block]  9.57 us
    dot_general x1, matrix products, local(): jnp.einsum('qd,skrd->kqsr', question_unit_vectors, arrived, preferred_ele...  8.48 us
    reduce_sum x2, other arithmetic, normalize(): jnp.sum(values * values, axis=-1, keepdims=True) + norm_epsilon  6.69 us
    all_to_all x1, starting transfers between devices, local(): lax.all_to_all(requests, 'grp', split_axis=0, concat_axis=0, tiled=True)  6.35 us
  transfers between devices with their start and end apart: 3, of which 1 were waited for; matrix products, arithmetic and copies ran while one was open for 12% of the time, Pallas kernels for 0%

profile of v1, /device:TPU:0, one launch (start us, length us, event | category | flops | bytes accessed | tf_op | source)
XLA Modules:
  0.0 310.3 jit_solution(13518792082319401792)
XLA Ops:
  0.6 0.7 fusion.21
  1.3 0.7 and_select_fusion
  2.0 0.2 convert_reduce_fusion
  2.2 0.7 fusion.22
  2.8 1.1 scatter_fusion
  4.0 0.7 copy.22
  4.6 6.4 %all-to-all-start = ((s32[8,1,2]{2,1,0:T(1,128)}), s32[8,1,2]{2,1,0:T(1,128)S(1)}, u32[]{:S(2)}, u32[]{:S(2)}) async-start(s32[8,1,2]{2,1,0:T(1,128)} %copy.22), calls=%async_computation | async-start | bytes 8192 | tf_op jit(solution)/shard_map/all_to_all | solution.py:56
  11.0 6.2 %fusion = f32[2048]{0:T(1024)S(1)} fusion(bf16[2048,2560]{1,0:T(8,128)(2,1)} %param.7), kind=kLoop, calls=%fused_computation.5 | loop fusion | flops 15726592 | bytes 10493952 | tf_op jit(solution)/shard_map/reduce_sum | solution.py:14
  17.2 0.7 copy-done
  17.9 5.5 %fusion.1 = bf16[2048,2560]{1,0:T(8,128)(2,1)} fusion(bf16[2048,2560]{1,0:T(8,128)(2,1)S(1)} %copy-done, f32[2048]{0:T(1024)S(1)} %add_rsqrt_fusion), kind=kLoop, calls=%fused_computation.6 | loop fusion | flops 15728640 | bytes 20979712 | tf_op jit(solution)/shard_map/convert_element_type | solution.py:15
  23.5 0.2 select_reduce_fusion.1
  23.8 0.7 copy.25
  24.6 5.1 %all-to-all-start.1 = ((s32[8,1,2]{2,1,0:T(1,128)}), s32[8,1,2]{2,1,0:T(1,128)S(1)}, u32[]{:S(2)}, u32[]{:S(2)}) async-start(s32[8,1,2]{2,1,0:T(1,128)} %copy.25), calls=%async_computation.1 | async-start | bytes 8192 | tf_op jit(solution)/shard_map/all_to_all | solution.py:66
  29.7 9.6 %gather_fusion = bf16[16,128,2560]{2,1,0:T(8,128)(2,1)} fusion(bf16[16,128,2560]{2,1,0:T(8,128)(2,1)} %bitcast.68, s32[1024]{0:T(1024)S(1)} %pad_clamp_fusion), kind=kCustom, calls=%fused_computation | custom fusion | bytes 20971584 | tf_op jit(solution)/shard_map/gather | solution.py:64
  39.3 5.3 %all-to-all-start.2 = ((bf16[8,2,128,2560]{3,2,1,0:T(8,128)(2,1)}), bf16[8,2,128,2560]{3,2,1,0:T(8,128)(2,1)}, u32[]{:S(2)}, u32[]{:S(2)}) async-start(bf16[8,2,128,2560]{3,2,1,0:T(8,128)(2,1)} %bitcast.69), calls=%async_computation.2 | async-start | bytes 20971520 | tf_op jit(solution)/shard_map/all_to_all | solution.py:65
  44.7 0.5 fusion.2
  45.2 9.9 %select_reduce_fusion = (f32[384]{0:T(512)S(1)}, f32[384,2048]{1,0:T(8,128)}) fusion(pred[2048]{0:T(1024)(128)(4,1)S(1)} %fusion.11, bf16[2048,2560]{1,0:T(8,128)(2,1)} %fusion.1, bf16[384,2560]{1,0:T(8,128)(2,1)S(1)} %copy-done.1, f32[384]{0:T(512)S(1)} %add_rsqrt_fusion.1), kind=kOutput, calls=%fused_computation.13 | convolution fusion | flops 4031839744 | bytes 15602688 | tf_op jit(solution)/shard_map/dot_general | solution.py:31
  55.1 5.2 %gather_fusion.1 = f32[384]{0:T(512)S(1)} fusion(f32[384,2048]{1,0:T(8,128)} %get-tuple-element.14, s32[384]{0:T(512)S(1)} %fusion.19), kind=kCustom, calls=%fused_computation.1 | custom fusion | bytes 6144 | tf_op jit(solution)/shard_map/jit(take_along_axis)/gather | solution.py:42
  60.4 0.1 copy.27
  60.6 212.8 %all-to-all-done.2 = bf16[8,2,128,2560]{3,2,1,0:T(8,128)(2,1)} async-done(((bf16[8,2,128,2560]{3,2,1,0:T(8,128)(2,1)}), bf16[8,2,128,2560]{3,2,1,0:T(8,128)(2,1)}, u32[]{:S(2)}, u32[]{:S(2)}) %all-to-all-start.2) | async-done | bytes 10485792 | tf_op jit(solution)/shard_map/all_to_all | solution.py:65
  273.4 8.5 %fusion.4 = f32[384]{0:T(512)S(1)} fusion(pred[2,8,128]{2,0,1:T(4,128)(4,1)S(1)} %iota_compare_fusion.2, bf16[8,2,128,2560]{3,2,1,0:T(8,128)(2,1)} %all-to-all-done.2, bf16[384,2560]{1,0:T(8,128)(2,1)S(1)} %copy-done.1, f32[384]{0:T(512)S(1)} %add_rsqrt_fusion.1), kind=kOutput, calls=%fused_computation.12 | convolution fusion | flops 4031839744 | bytes 12456960 | tf_op jit(solution)/shard_map/qd,skrd->kqsr/dot_general | solution.py:68
  281.9 1.2 fusion.24
  283.1 10.6 %all-reduce.1 = (f32[]{:T(128)}, f32[]{:T(128)}) all-reduce(f32[]{:T(128)} %get-tuple-element.3, f32[]{:T(128)} %get-tuple-element.2), channel_id=1, replica_groups=mesh['grp'=8,'rep'=4] {'rep'}, use_global_device_ids=true, to_apply=%region_8.9 | all-reduce | flops 2 | bytes 16 | tf_op jit(solution)/shard_map/psum | solution.py:79
  293.7 14.2 %all-reduce = (f32[]{:T(128)}, f32[]{:T(128)}) all-reduce(f32[]{:T(128)} %get-tuple-element.6, f32[]{:T(128)} %get-tuple-element.7), channel_id=1, replica_groups=mesh['grp'=8,'rep'=4] {'grp'}, use_global_device_ids=true, to_apply=%region_9.10 | all-reduce | flops 2 | bytes 16 | tf_op jit(solution)/shard_map/psum | solution.py:78
  (28 shorter events, 0.6 us)
Async XLA Ops:
  4.6 18.8 %all-to-all-start = ((s32[8,1,2]{2,1,0:T(1,128)}), s32[8,1,2]{2,1,0:T(1,128)S(1)}, u32[]{:S(2)}, u32[]{:S(2)}) async-start(s32[8,1,2]{2,1,0:T(1,128)} %copy.22), calls=%async_computation | async-start | bytes 8192 | tf_op jit(solution)/shard_map/all_to_all | solution.py:56
  11.0 7.0 %copy-start = (bf16[2048,2560]{1,0:T(8,128)(2,1)S(1)}, bf16[2048,2560]{1,0:T(8,128)(2,1)}, u32[]{:S(2)}) copy-start(bf16[2048,2560]{1,0:T(8,128)(2,1)} %param.7) | copy-start | bytes 31457284
  17.9 5.6 %copy-start.3 = (s32[16]{0:T(128)S(1)}, s32[16]{0:T(128)}, u32[]{:S(2)}) copy-start(s32[16]{0:T(128)} %param.8) | copy-start | bytes 196
  24.6 14.7 %all-to-all-start.1 = ((s32[8,1,2]{2,1,0:T(1,128)}), s32[8,1,2]{2,1,0:T(1,128)S(1)}, u32[]{:S(2)}, u32[]{:S(2)}) async-start(s32[8,1,2]{2,1,0:T(1,128)} %copy.25), calls=%async_computation.1 | async-start | bytes 8192 | tf_op jit(solution)/shard_map/all_to_all | solution.py:66
  39.3 5.3 %copy-start.2 = (s32[384]{0:T(512)S(1)}, s32[384]{0:T(512)}, u32[]{:S(2)}) copy-start(s32[384]{0:T(512)} %param.9) | copy-start | bytes 4612
  39.3 5.5 %copy-start.1 = (bf16[384,2560]{1,0:T(8,128)(2,1)S(1)}, bf16[384,2560]{1,0:T(8,128)(2,1)}, u32[]{:S(2)}) copy-start(bf16[384,2560]{1,0:T(8,128)(2,1)} %param.6) | copy-start | bytes 5898244
  39.3 234.1 %all-to-all-start.2 = ((bf16[8,2,128,2560]{3,2,1,0:T(8,128)(2,1)}), bf16[8,2,128,2560]{3,2,1,0:T(8,128)(2,1)}, u32[]{:S(2)}, u32[]{:S(2)}) async-start(bf16[8,2,128,2560]{3,2,1,0:T(8,128)(2,1)} %bitcast.69), calls=%async_computation.2 | async-start | bytes 20971520 | tf_op jit(solution)/shard_map/all_to_all | solution.py:65
  60.6 221.3 %copy-start.4 = (f32[384]{0:T(512)S(1)}, f32[384]{0:T(512)}, u32[]{:S(2)}) copy-start(f32[384]{0:T(512)} %param.11) | copy-start | bytes 4612
